TPU v7x, 256 devices: a whole 4x4x8 slice. The times are simulated.
256 devices in a mesh: mem: 32 (over z, x), lon: 4 (over y), lat: 2 (over core).
Axes of the slice: x: 4, y: 4, z: 8, core: 2. Of those that a mesh axis runs over, the one named last changes fastest.
Arguments:
- ens_obs: bfloat16 [1024, 8, 16, 128], P('mem', 'lat', 'lon'), may hold values from -16 to 16
- innovation: bfloat16 [8, 16, 128], P('lat', 'lon'), may hold values from -6 to 6
- obs_weight: bfloat16 [8, 16, 128], P('lat', 'lon'), may hold values from 0.5 to 5
- loc_list: int32 [32, 8, 4], P(None, ('lon', 'lat')), may hold values from 0 to 47, as said below
- counts: int32 [32, 8], P('mem', ('lon', 'lat')), may hold values from 1 to 4, as said below
- taper: float32 [32, 8, 4], P('mem', ('lon', 'lat')), may hold values from 0.2 to 1
- state: bfloat16 [1024, 32, 8, 1280], P('mem', None, ('lon', 'lat')), may hold values from -6 to 6
Outputs:
- analysis: bfloat16 [1024, 32, 8, 1280], P('mem', None, ('lon', 'lat'))
Inputs may be any that keep to these rules, and one draw needn't show every extreme that they name: `loc_list`: the 4 entries of a patch name different window blocks; only the first counts entries are used. `counts`: some patch uses all 4 listed blocks in every draw.
All inputs are finite; a program needn't handle non-finite values.
Results may differ from a plain program's by a relative error of at most 0.0068.
Values may be sent and summed in bfloat16 or wider, within the bound.
A program may use at most 64 MiB of HBM per device.

v0:
```python
import jax
import jax.numpy as jnp
from jax import lax
from jax.sharding import PartitionSpec as P

NSI = 2


def padded(block, sides, width):
    for axis, dim in sides:
        count = lax.axis_size(axis)
        forward = [(i, i + 1) for i in range(count - 1)]
        forward.append((count - 1, 0))
        backward = [(target, source) for source, target in forward]
        low = lax.ppermute(
            lax.slice_in_dim(block, block.shape[dim] - width, None, axis=dim), axis, forward
        )
        high = lax.ppermute(lax.slice_in_dim(block, 0, width, axis=dim), axis, backward)
        block = jnp.concatenate([low, block, high], axis=dim)
    return block


def inverse_root(start_low):
    member_total = start_low.shape[0]
    identity = jnp.eye(member_total, dtype=jnp.float32)
    upper_iter = start_low
    lower_iter = start_low
    for sweep_index in range(NSI):
        if sweep_index == 0:
            product = start_low.astype(jnp.float32)
        else:
            product = jnp.dot(lower_iter, upper_iter, preferred_element_type=jnp.float32)
        halfstep = 0.5 * (3.0 * identity - product)
        half_low = halfstep.astype(jnp.bfloat16)
        if sweep_index == NSI - 1:
            return jnp.dot(half_low, lower_iter, preferred_element_type=jnp.float32)
        next_upper = jnp.dot(upper_iter, half_low, preferred_element_type=jnp.float32).astype(
            jnp.bfloat16
        )
        lower_iter = half_low
        upper_iter = next_upper


def weights_from_gram(gram_mat, drive_vec):
    member_total = gram_mat.shape[0]
    divisor = float(member_total - 1)
    identity = jnp.eye(member_total, dtype=jnp.float32)
    a_matrix = identity + gram_mat / divisor
    trace_level = 2.0 * jnp.trace(a_matrix) / member_total
    start_low = lax.optimization_barrier((a_matrix / trace_level).astype(jnp.bfloat16))
    inv_root = (inverse_root(start_low) / jnp.sqrt(trace_level)).astype(jnp.bfloat16)
    inner_vec = jnp.dot(
        inv_root, (drive_vec / divisor).astype(jnp.bfloat16), preferred_element_type=jnp.float32
    )
    mean_weights = jnp.dot(
        inv_root, inner_vec.astype(jnp.bfloat16), preferred_element_type=jnp.float32
    )
    return (inv_root.astype(jnp.float32) + mean_weights[:, None]).astype(jnp.bfloat16)


def on_device(ens_obs, innovation, obs_weight, loc_list, counts, taper, state):
    local_members, band_rows, band_cols, block_len = ens_obs.shape
    group_patches = loc_list.shape[0]
    slot_count = loc_list.shape[2]
    own_count = taper.shape[0]
    state_len = state.shape[3]
    stacked = jnp.concatenate([ens_obs, innovation[None], obs_weight[None]], axis=0)
    framed = padded(stacked, (("lon", 2),), band_cols)
    window = framed.reshape(local_members + 2, band_rows * 3 * band_cols, block_len)
    picked = window[:, loc_list[:, 0, :], :]
    ens_part = picked[:local_members].reshape(local_members, group_patches, slot_count * block_len)
    first_slot = lax.axis_index("mem") * own_count
    own_side = jnp.moveaxis(
        lax.dynamic_slice_in_dim(picked[local_members:], first_slot, own_count, 1), 1, 0
    )
    flat_state = state.reshape(local_members, group_patches, state_len)
    ens_full = lax.all_to_all(ens_part, "mem", split_axis=1, concat_axis=0, tiled=True)

    def patch_weights(inputs):
        patch_index, tapers, live_count, obs_side = inputs
        selected = lax.dynamic_index_in_dim(ens_full, patch_index, 1, keepdims=False)
        live_mask = (jnp.arange(slot_count, dtype=jnp.int32) < live_count).astype(jnp.float32)
        obs_factor = obs_side[1].astype(jnp.float32) * (tapers * live_mask)[:, None]
        weighted = (selected * obs_factor.reshape(-1)).astype(jnp.bfloat16)
        gram_mat = lax.dot_general(
            weighted, selected, (((1,), (1,)), ((), ())), preferred_element_type=jnp.float32
        )
        drive_vec = jnp.dot(weighted, obs_side[0].reshape(-1), preferred_element_type=jnp.float32)
        return weights_from_gram(gram_mat, drive_vec)

    weight_stack = lax.map(
        patch_weights,
        (jnp.arange(own_count, dtype=jnp.int32), taper[:, 0, :], counts[:, 0], own_side),
    )
    state_full = lax.all_to_all(flat_state, "mem", split_axis=1, concat_axis=0, tiled=True)
    analysis_own = jnp.einsum(
        "pkj,kps->jps", weight_stack, state_full, preferred_element_type=jnp.float32
    ).astype(jnp.bfloat16)
    returned = lax.all_to_all(analysis_own, "mem", split_axis=0, concat_axis=1, tiled=True)
    return returned.reshape(local_members, group_patches, 1, state_len)


def solution(mesh):
    return jax.shard_map(
        on_device,
        mesh=mesh,
        in_specs=(
            P("mem", "lat", "lon", None),
            P("lat", "lon", None),
            P("lat", "lon", None),
            P(None, ("lon", "lat"), None),
            P("mem", ("lon", "lat")),
            P("mem", ("lon", "lat"), None),
            P("mem", None, ("lon", "lat"), None),
        ),
        out_specs=P("mem", None, ("lon", "lat"), None),
        check_vma=False,
    )
```

profile of v0, /device:TPU:8, one launch (start us, length us, event | category | flops | bytes accessed | tf_op | source)
XLA Modules:
  0.0 211.1 jit_solution(16215918792205847067)
XLA Ops:
  0.0 1.0 pad_maximum_fusion.1
  1.0 2.3 %collective-permute-start.1 = (bf16[34,4,4,128]{3,2,1,0:T(4,128)(2,1)S(1)}, bf16[34,4,4,128]{3,2,1,0:T(4,128)(2,1)S(1)}, u32[]{:S(2)}, u32[]{:S(2)}) collective-permute-start(bf16[34,4,4,128]{3,2,1,0:T(4,128)(2,1)S(1)} %pad_maximum_fusion.1), channel_id=1, source_target_pairs={{2,0},{4,2},{6,4},{0,6},{3,1},{5,3},{7,5},{1,7},{10,8},{12,10},{14... | collective-permute-start | bytes 417800 | tf_op jit(solution)/shard_map/ppermute | solution.py:18
  3.3 0.0 collective-permute-start
  3.3 0.7 compare_select_fusion
  4.0 0.1 copy.29
  4.1 0.1 reshape.102
  4.2 2.3 %collective-permute-done.1 = bf16[34,4,4,128]{3,2,1,0:T(4,128)(2,1)S(1)} collective-permute-done((bf16[34,4,4,128]{3,2,1,0:T(4,128)(2,1)S(1)}, bf16[34,4,4,128]{3,2,1,0:T(4,128)(2,1)S(1)}, u32[]{:S(2)}, u32[]{:S(2)}) %collective-permute-start.1) | collective-permute-done | bytes 139296 | tf_op jit(solution)/shard_map/ppermute | solution.py:18
  6.5 1.8 collective-permute-done
  8.4 1.2 pad_maximum_fusion
  9.6 0.3 copy.28
  9.9 0.8 gather_fusion
  10.7 0.6 copy.40
  11.3 0.6 slice.22
  11.9 0.4 reshape.115
  12.4 1.5 copy.35
  13.9 10.9 %all-to-all-start = ((bf16[32,32,512]{2,0,1:T(8,128)(2,1)}), bf16[32,32,512]{2,0,1:T(8,128)(2,1)S(1)}, u32[]{:S(2)}, u32[]{:S(2)}) async-start(bf16[32,32,512]{2,0,1:T(8,128)(2,1)} %copy.35), calls=%async_computation | async-start | bytes 2097152 | tf_op jit(solution)/shard_map/all_to_all | solution.py:77
  24.9 4.7 %copy.39 = bf16[32,32,1,1280]{3,0,1,2:T(8,128)(2,1)} copy(bf16[32,32,1,1280]{3,1,2,0:T(8,128)(2,1)} %param.13) | data formatting | bytes 5242880 | tf_op args[6]
  29.6 22.5 %all-to-all-done = bf16[32,32,512]{2,0,1:T(8,128)(2,1)S(1)} async-done(((bf16[32,32,512]{2,0,1:T(8,128)(2,1)}), bf16[32,32,512]{2,0,1:T(8,128)(2,1)S(1)}, u32[]{:S(2)}, u32[]{:S(2)}) %all-to-all-start) | async-done | bytes 1048608 | tf_op jit(solution)/shard_map/all_to_all | solution.py:77
  52.1 0.0 copy-start.1
  52.1 6.0 %all-to-all-start.1 = ((bf16[32,32,1280]{2,0,1:T(8,128)(2,1)}), bf16[32,32,1280]{2,0,1:T(8,128)(2,1)}, u32[]{:S(2)}, u32[]{:S(2)}) async-start(bf16[32,32,1280]{2,0,1:T(8,128)(2,1)} %bitcast.59), calls=%async_computation.1 | async-start | bytes 5242880 | tf_op jit(solution)/shard_map/all_to_all | solution.py:95
  58.7 0.0 copy-done.1
  58.8 0.1 convert_multiply_fusion
  58.9 0.2 multiply_convert_fusion
  59.1 0.4 fusion.32
  59.5 3.8 %select_reduce_fusion = (f32[]{:T(128)}, f32[1024,1024]{1,0:T(8,128)}) fusion(bf16[1024,512]{1,0:T(8,128)(2,1)S(1)} %bitcast.69, bf16[1024,512]{1,0:T(8,128)(2,1)S(1)} %bitcast.67), kind=kOutput, calls=%fused_computation.10 | convolution fusion | flops 1080033280 | bytes 6291460 | tf_op jit(solution)/shard_map/while/body/eval_jaxpr/dot_general | solution.py:85
  64.0 2.8 %divide_convert_fusion.1 = bf16[1024,1024]{1,0:T(8,128)(2,1)S(1)} fusion(f32[1024,1024]{1,0:T(8,128)} %get-tuple-element.16, f32[]{:T(128)S(6)} %div.29), kind=kLoop, calls=%fused_computation.9 | loop fusion | flops 6291456 | bytes 6291460 | tf_op jit(solution)/shard_map/while/body/eval_jaxpr/convert_element_type | solution.py:50
  66.8 0.0 copy-start
  66.8 1.3 copy-done
  68.1 3.7 %fusion.21 = bf16[1024,1024]{1,0:T(8,128)(2,1)} fusion(bf16[1024,1024]{1,0:T(8,128)(2,1)S(1)} %divide_convert_fusion.1), kind=kOutput, calls=%fused_computation.24 | convolution fusion | flops 2153775104 | bytes 4194304 | tf_op jit(solution)/shard_map/while/body/eval_jaxpr/dot_general | solution.py:37
  71.8 7.4 %divide_convert_fusion = bf16[1024,1024]{1,0:T(8,128)(2,1)S(1)} fusion(f32[]{:T(128)S(6)} %sqrt.4, bf16[1024,1024]{1,0:T(8,128)(2,1)} %fusion.21, bf16[1024,1024]{1,0:T(8,128)(2,1)} %copy-done), kind=kOutput, calls=%fused_computation.8 | convolution fusion | flops 4314890240 | bytes 6291460 | tf_op jit(solution)/shard_map/while/body/eval_jaxpr/dot_general | solution.py:36
  79.2 0.6 fusion.33
  79.8 0.6 fusion.34
  80.5 37.3 %all-to-all-done.1 = bf16[32,32,1280]{2,0,1:T(8,128)(2,1)} async-done(((bf16[32,32,1280]{2,0,1:T(8,128)(2,1)}), bf16[32,32,1280]{2,0,1:T(8,128)(2,1)}, u32[]{:S(2)}, u32[]{:S(2)}) %all-to-all-start.1) | async-done | bytes 2621472 | tf_op jit(solution)/shard_map/all_to_all | solution.py:95
  117.8 6.1 %fusion.4 = bf16[1024,1,1280]{2,0,1:T(8,128)(2,1)} fusion(bf16[1024,1280]{1,0:T(8,128)(2,1)} %bitcast.22, bf16[1024,1024]{1,0:T(8,128)(2,1)S(1)} %divide_convert_fusion, f32[1024]{0:T(1024)S(1)} %bitcast.76), kind=kOutput, calls=%fused_computation.14 | convolution fusion | flops 2688811008 | bytes 7344128 | tf_op jit(solution)/shard_map/pkj,kps->jps/dot_general | solution.py:96
  123.9 0.5 broadcast.106
  124.4 4.4 %reduce = bf16[1024,1280]{1,0:T(8,128)(2,1)S(1)} reduce(bf16[1024,1,1280]{2,0,1:T(8,128)(2,1)} %fusion.4, bf16[]{:T(256)} %broadcast.106), dimensions={1}, to_apply=%copy.33.reduce_sub_computation | reduce | bytes 5242882 | tf_op jit(solution)/shard_map/convert_element_type | solution.py:98
  128.9 2.2 %reshape.116 = bf16[32,2,20480]{2,1,0:T(2,128)(2,1)} reshape(bf16[1024,1280]{1,0:T(8,128)(2,1)S(1)} %reduce) | data formatting | bytes 5242880
  131.1 67.0 %all_to_all.45 = bf16[32,2,20480]{2,1,0:T(2,128)(2,1)S(1)} all-to-all(bf16[32,2,20480]{2,1,0:T(2,128)(2,1)} %reshape.116), channel_id=1, replica_groups=mesh['mem'=32,'lon'=4,'lat'=2] {'mem'}, dimensions={0} | all-to-all | bytes 5242880 | tf_op jit(solution)/shard_map/all_to_all | solution.py:99
  198.0 7.2 %reshape.117 = bf16[1024,1,1280]{2,1,0:T(2,128)(2,1)} reshape(bf16[32,2,20480]{2,1,0:T(2,128)(2,1)S(1)} %all_to_all.45) | data formatting | bytes 5242880
  205.2 2.9 %copy.36 = bf16[1024,1,1280]{2,0,1:T(8,128)(2,1)S(1)} copy(bf16[1024,1,1280]{2,1,0:T(2,128)(2,1)} %reshape.117) | data formatting | bytes 5242880
  208.1 2.9 %copy.34 = bf16[32,32,1,1280]{3,1,2,0:T(8,128)(2,1)} copy(bf16[32,32,1,1280]{3,0,1,2:T(8,128)(2,1)S(1)} %bitcast.62) | data formatting | bytes 5242880 | tf_op jit(solution)/shard_map/all_to_all | solution.py:99
  (9 shorter events, 0.1 us)
Async XLA Ops:
  1.0 5.5 %collective-permute-start.1 = (bf16[34,4,4,128]{3,2,1,0:T(4,128)(2,1)S(1)}, bf16[34,4,4,128]{3,2,1,0:T(4,128)(2,1)S(1)}, u32[]{:S(2)}, u32[]{:S(2)}) collective-permute-start(bf16[34,4,4,128]{3,2,1,0:T(4,128)(2,1)S(1)} %pad_maximum_fusion.1), channel_id=1, source_target_pairs={{2,0},{4,2},{6,4},{0,6},{3,1},{5,3},{7,5},{1,7},{10,8},{12,10},{14... | collective-permute-start | bytes 417800 | tf_op jit(solution)/shard_map/ppermute | solution.py:18
  3.3 5.1 %collective-permute-start = (bf16[34,4,4,128]{3,2,1,0:T(4,128)(2,1)S(1)}, bf16[34,4,4,128]{3,2,1,0:T(4,128)(2,1)S(1)}, u32[]{:S(2)}, u32[]{:S(2)}) collective-permute-start(bf16[34,4,4,128]{3,2,1,0:T(4,128)(2,1)S(1)} %pad_maximum_fusion.1), channel_id=1, source_target_pairs={{0,2},{2,4},{4,6},{6,0},{1,3},{3,5},{5,7},{7,1},{8,10},{10,12},{12... | collective-permute-start | bytes 417800 | tf_op jit(solution)/shard_map/ppermute | solution.py:15
  13.9 38.1 %all-to-all-start = ((bf16[32,32,512]{2,0,1:T(8,128)(2,1)}), bf16[32,32,512]{2,0,1:T(8,128)(2,1)S(1)}, u32[]{:S(2)}, u32[]{:S(2)}) async-start(bf16[32,32,512]{2,0,1:T(8,128)(2,1)} %copy.35), calls=%async_computation | async-start | bytes 2097152 | tf_op jit(solution)/shard_map/all_to_all | solution.py:77
  52.1 6.7 %copy-start.1 = (f32[1,1,4]{2,1,0:T(1,128)S(1)}, f32[1,1,4]{2,1,0:T(1,128)}, u32[]{:S(2)}) copy-start(f32[1,1,4]{2,1,0:T(1,128)} %param.12) | copy-start | bytes 52
  52.1 65.7 %all-to-all-start.1 = ((bf16[32,32,1280]{2,0,1:T(8,128)(2,1)}), bf16[32,32,1280]{2,0,1:T(8,128)(2,1)}, u32[]{:S(2)}, u32[]{:S(2)}) async-start(bf16[32,32,1280]{2,0,1:T(8,128)(2,1)} %bitcast.59), calls=%async_computation.1 | async-start | bytes 5242880 | tf_op jit(solution)/shard_map/all_to_all | solution.py:95
  66.8 1.3 copy-start
where the time goes:
time: 212 us; the launch traced here: 211 us
  blocking collectives  67 us (32%)
  waiting for transfers between devices  63.9 us (30%)
  local copies, waits for them, and re-layouts  26.3 us (12%)
  matrix products  22.7 us (11%)
  starting transfers between devices  19.2 us (9%)
  other arithmetic  10.5 us (5%)
    all_to_all x1, blocking collectives, on_device(): lax.all_to_all(analysis_own, 'mem', split_axis=0, concat_axis=1, tiled=True)  67 us
    all_to_all x1, waiting for transfers between devices, on_device(): lax.all_to_all(flat_state, 'mem', split_axis=1, concat_axis=0, tiled=True)  37.3 us
    all_to_all x1, waiting for transfers between devices, on_device(): lax.all_to_all(ens_part, 'mem', split_axis=1, concat_axis=0, tiled=True)  22.5 us
    unnamed x8, local copies, waits for them, and re-layouts  18.3 us
    all_to_all x1, starting transfers between devices, on_device(): lax.all_to_all(ens_part, 'mem', split_axis=1, concat_axis=0, tiled=True)  10.9 us
    dot_general x1, matrix products, inverse_root(): return jnp.dot(half_low, lower_iter, preferred_element_type=jnp.float32)  7.36 us
    dot_general x1, matrix products, on_device(): jnp.einsum('pkj,kps->jps', weight_stack, state_full, preferred_element_ty...  6.13 us
    all_to_all x1, starting transfers between devices, on_device(): lax.all_to_all(flat_state, 'mem', split_axis=1, concat_axis=0, tiled=True)  6.01 us
  transfers between devices with their start and end apart: 4, of which 4 were waited for; matrix products, arithmetic and copies ran while one was open for 12% of the time, Pallas kernels for 0%

commit v1 on v0

v1 whole, which is shorter than its diff:
```python
import functools

import jax
import jax.numpy as jnp
from jax import lax
from jax.experimental import pallas as pl
from jax.experimental.pallas import tpu as pltpu
from jax.sharding import PartitionSpec as P

MESH = pl.DeviceIdType.MESH
ZN, XN, YN = 8, 4, 4
PEERS = ZN * XN
ROWS = 32
MEMBERS = 1024
OBS = 512
BLK = 128
SLOTS = 4
SDIM = 1280
TILE = 256
SELF_STEP = 4


def kernel(
    obs_ref, side_ref, loc_ref, cnt_ref, tap_ref, state_ref, out_ref,
    win, wside, pick, xfull, wgt, sfull, yroot, zroot, ynext, wmat, omat,
    halo_send, halo_recv, side_send, side_recv,
    ens_send, ens_recv, st_send, st_recv, out_send, out_recv, loc_sem,
):
    me = lax.axis_index("mem")
    zc, xc = me // XN, me % XN
    yc = lax.axis_index("lon")

    def peer(dz, dx):
        return ((zc + dz) % ZN) * XN + (xc + dx) % XN

    def offset(k):
        dz = (4 + 3 * (k % ZN)) % ZN
        return dz, (k // ZN + dz) % XN

    y_up, y_down = (yc + 1) % YN, (yc + YN - 1) % YN

    barrier = pltpu.get_barrier_semaphore()

    def greet(k, carry):
        dz, dx = offset(k)
        pl.semaphore_signal(
            barrier, inc=1, device_id={"mem": peer(dz, dx)}, device_id_type=MESH
        )
        return carry

    lax.fori_loop(0, SELF_STEP, greet, 0)
    lax.fori_loop(SELF_STEP + 1, PEERS, greet, 0)
    for other in (y_up, y_down):
        pl.semaphore_signal(barrier, inc=1, device_id={"lon": other}, device_id_type=MESH)
    pl.semaphore_wait(barrier, PEERS - 1 + 2)

    halo = []
    for slot, other in ((0, y_up), (2, y_down)):
        i = slot // 2
        halo.append(
            pltpu.make_async_remote_copy(
                src_ref=obs_ref, dst_ref=win.at[slot],
                send_sem=halo_send.at[i], recv_sem=halo_recv.at[i],
                device_id={"lon": other}, device_id_type=MESH,
            )
        )
        halo.append(
            pltpu.make_async_remote_copy(
                src_ref=side_ref, dst_ref=wside.at[slot],
                send_sem=side_send.at[i], recv_sem=side_recv.at[i],
                device_id={"lon": other}, device_id_type=MESH,
            )
        )
    for copy in halo:
        copy.start()

    my_rows = pl.ds(pl.multiple_of(me * ROWS, ROWS), ROWS)

    def state_copy(k):
        dz, dx = offset(k)
        to = peer(dz, dx)
        return pltpu.make_async_remote_copy(
            src_ref=state_ref.at[to], dst_ref=sfull.at[my_rows],
            send_sem=st_send.at[k], recv_sem=st_recv.at[k],
            device_id={"mem": to}, device_id_type=MESH,
        )

    def ens_copy(k):
        dz, dx = offset(k)
        to = peer(dz, dx)
        return pltpu.make_async_remote_copy(
            src_ref=pick.at[to], dst_ref=xfull.at[my_rows],
            send_sem=ens_send.at[k], recv_sem=ens_recv.at[k],
            device_id={"mem": to}, device_id_type=MESH,
        )

    def start(make):
        def body(k, carry):
            make(k).start()
            return carry
        return body

    def wait_recv(make):
        def body(k, carry):
            make(k).wait_recv()
            return carry
        return body

    def wait_send(make):
        def body(k, carry):
            make(k).wait_send()
            return carry
        return body

    def others(body):
        lax.fori_loop(0, SELF_STEP, body, 0)
        lax.fori_loop(SELF_STEP + 1, PEERS, body, 0)

    own_state = pltpu.make_async_copy(state_ref.at[me], sfull.at[my_rows], loc_sem.at[0])
    own_state.start()
    lax.fori_loop(0, SELF_STEP, start(state_copy), 0)

    win[1] = obs_ref[...]
    wside[1] = side_ref[...]
    for copy in halo:
        copy.wait()

    def block_index(number):
        row = (number * 43) >> 9
        col = number - row * 12
        group = col >> 2
        return group, row * 4 + (col - group * 4)

    def pick_patch(p, carry):
        for j in range(SLOTS):
            group, block = block_index(loc_ref[p * SLOTS + j])
            pick[p, :, j * BLK : (j + 1) * BLK] = win[group, block]
        return carry

    lax.fori_loop(0, PEERS, pick_patch, 0)
    others(start(ens_copy))
    xfull[my_rows, :] = pick[me]
    lax.fori_loop(SELF_STEP + 1, PEERS, start(state_copy), 0)

    count = cnt_ref[0]
    factors, innovs = [], []
    for j in range(SLOTS):
        group, block = block_index(loc_ref[me * SLOTS + j])
        level = jnp.where(j < count, tap_ref[j], 0.0)
        innovs.append(wside[group, pl.ds(block, 1), :])
        factors.append(wside[group, pl.ds(block + 16, 1), :] * level)
    factor = jnp.concatenate(factors, axis=1)
    innov = jnp.concatenate(innovs, axis=1)

    others(wait_recv(ens_copy))

    drives = []
    total = jnp.zeros((1, 1), jnp.float32)
    for t in range(MEMBERS // TILE):
        rows = pl.ds(t * TILE, TILE)
        selected = xfull[rows, :].astype(jnp.float32)
        weighted = (selected * factor).astype(jnp.bfloat16)
        wgt[rows, :] = weighted
        weighted = weighted.astype(jnp.float32)
        drives.append(jnp.sum(weighted * innov, axis=1, keepdims=True))
        total += jnp.sum(
            jnp.sum(weighted * selected, axis=1, keepdims=True), axis=0, keepdims=True
        )
    divisor = float(MEMBERS - 1)
    level = 2.0 + total * (2.0 / (divisor * MEMBERS))
    inv_level = 1.0 / level
    inv_sqrt = 1.0 / jnp.sqrt(level)

    def eye(t):
        row = lax.broadcasted_iota(jnp.int32, (TILE, MEMBERS), 0) + t * TILE
        col = lax.broadcasted_iota(jnp.int32, (TILE, MEMBERS), 1)
        return jnp.where(row == col, 1.0, 0.0).astype(jnp.float32)

    def tile_rows(t):
        return pl.ds(pl.multiple_of(t * TILE, TILE), TILE)

    def gram_step(t, carry):
        rows = tile_rows(t)
        gram = lax.dot_general(
            wgt[rows, :], xfull[...], (((1,), (1,)), ((), ())),
            preferred_element_type=jnp.float32,
        )
        unit = eye(t)
        low = ((unit + gram * (1.0 / divisor)) * inv_level).astype(jnp.bfloat16)
        yroot[rows, :] = low
        zroot[rows, :] = (0.5 * (3.0 * unit - low.astype(jnp.float32))).astype(jnp.bfloat16)
        return carry

    lax.fori_loop(0, MEMBERS // TILE, gram_step, 0)

    def y_step(t, carry):
        rows = tile_rows(t)
        ynext[rows, :] = jnp.dot(
            yroot[rows, :], zroot[...], preferred_element_type=jnp.float32
        ).astype(jnp.bfloat16)
        return carry

    lax.fori_loop(0, MEMBERS // TILE, y_step, 0)

    def root_step(t, carry):
        rows = tile_rows(t)
        product = jnp.dot(zroot[rows, :], ynext[...], preferred_element_type=jnp.float32)
        half = (0.5 * (3.0 * eye(t) - product)).astype(jnp.bfloat16)
        last = jnp.dot(half, zroot[...], preferred_element_type=jnp.float32)
        yroot[rows, :] = (last * inv_sqrt).astype(jnp.bfloat16)
        return carry

    lax.fori_loop(0, MEMBERS // TILE, root_step, 0)

    drive = jnp.concatenate(drives, axis=0) * (1.0 / divisor)
    drive = jnp.broadcast_to(drive, (MEMBERS, BLK)).astype(jnp.bfloat16)
    inner = jnp.dot(yroot[...], drive, preferred_element_type=jnp.float32)
    mean = jnp.dot(yroot[...], inner.astype(jnp.bfloat16), preferred_element_type=jnp.float32)
    for t in range(MEMBERS // TILE):
        rows = pl.ds(t * TILE, TILE)
        full = yroot[rows, :].astype(jnp.float32) + mean[t * TILE : (t + 1) * TILE, 0:1]
        wmat[:, t * TILE : (t + 1) * TILE] = full.T.astype(jnp.bfloat16)

    others(wait_recv(state_copy))
    own_state.wait()

    def out_copy(k, dz, dx):
        to = peer(dz, dx)
        return pltpu.make_async_remote_copy(
            src_ref=omat.at[pl.ds(pl.multiple_of(to * ROWS, ROWS), ROWS)],
            dst_ref=out_ref.at[me],
            send_sem=out_send.at[k], recv_sem=out_recv.at[k],
            device_id={"mem": to}, device_id_type=MESH,
        )

    plane = XN * ROWS
    sends = []
    for pair in ((4, 3), (5, 2), (6, 1), (7, 0)):
        starts = [pl.multiple_of(((zc + dz) % ZN) * plane, plane) for dz in pair]
        left = jnp.concatenate([wmat[pl.ds(s, plane), :] for s in starts], axis=0)
        block = jnp.dot(left, sfull[...], preferred_element_type=jnp.float32)
        block = block.astype(jnp.bfloat16)
        for i, s in enumerate(starts):
            omat[pl.ds(s, plane), :] = block[i * plane : (i + 1) * plane, :]
        for dx in range(XN):
            for dz in pair:
                if dz or dx:
                    copy = out_copy(dz * XN + dx, dz, dx)
                    copy.start()
                    sends.append(copy)
    own_out = pltpu.make_async_copy(omat.at[my_rows], out_ref.at[me], loc_sem.at[1])
    own_out.start()

    others(wait_send(ens_copy))
    others(wait_send(state_copy))
    for copy in sends:
        copy.wait()
    own_out.wait()


def on_device(ens_obs, innovation, obs_weight, loc_list, counts, taper, state):
    local, rows, cols, blk = ens_obs.shape
    patches = loc_list.shape[0]
    obs = jnp.transpose(ens_obs, (1, 2, 0, 3)).reshape(rows * cols, local, blk)
    side = jnp.concatenate(
        [innovation.reshape(rows * cols, blk), obs_weight.reshape(rows * cols, blk)], axis=0
    ).astype(jnp.float32)
    by_patch = jnp.transpose(state.reshape(local, patches, SDIM), (1, 0, 2))
    vmem = pl.BlockSpec(memory_space=pltpu.VMEM)
    smem = pl.BlockSpec(memory_space=pltpu.SMEM)
    anywhere = pl.BlockSpec(memory_space=pl.ANY)
    dma = pltpu.SemaphoreType.DMA
    low = jnp.bfloat16
    out = pl.pallas_call(
        kernel,
        out_shape=jax.ShapeDtypeStruct((patches, local, SDIM), low),
        in_specs=[vmem, vmem, smem, smem, smem, anywhere],
        out_specs=anywhere,
        scratch_shapes=[
            pltpu.VMEM((3, rows * cols, local, blk), low),
            pltpu.VMEM((3, 2 * rows * cols, blk), jnp.float32),
            pltpu.VMEM((PEERS, local, OBS), low),
            pltpu.VMEM((MEMBERS, OBS), low),
            pltpu.VMEM((MEMBERS, OBS), low),
            pltpu.VMEM((MEMBERS, SDIM), low),
            pltpu.VMEM((MEMBERS, MEMBERS), low),
            pltpu.VMEM((MEMBERS, MEMBERS), low),
            pltpu.VMEM((MEMBERS, MEMBERS), low),
            pltpu.VMEM((MEMBERS, MEMBERS), low),
            pltpu.VMEM((MEMBERS, SDIM), low),
            dma((2,)), dma((2,)), dma((2,)), dma((2,)),
            dma((PEERS,)), dma((PEERS,)), dma((PEERS,)), dma((PEERS,)),
            dma((PEERS,)), dma((PEERS,)), dma((2,)),
        ],
        name="analysis",
        compiler_params=pltpu.CompilerParams(
            collective_id=0, has_side_effects=True, vmem_limit_bytes=56 << 20
        ),
    )(obs, side, loc_list.reshape(-1), counts.reshape(-1), taper.reshape(-1), by_patch)
    return jnp.transpose(out, (1, 0, 2)).reshape(local, patches, 1, SDIM)


def solution(mesh):
    return jax.shard_map(
        on_device,
        mesh=mesh,
        in_specs=(
            P("mem", "lat", "lon", None),
            P("lat", "lon", None),
            P("lat", "lon", None),
            P(None, ("lon", "lat"), None),
            P("mem", ("lon", "lat")),
            P("mem", ("lon", "lat"), None),
            P("mem", None, ("lon", "lat"), None),
        ),
        out_specs=P("mem", None, ("lon", "lat"), None),
        check_vma=False,
    )
```

time: 212 us -> 171 us (0.81)
  Pallas kernels: 0 us -> 155 us
  blocking collectives: 67 us -> 0 us
  waiting for transfers between devices: 63.9 us -> 0 us
  matrix products: 22.7 us -> 0 us
  starting transfers between devices: 19.2 us -> 0 us
  local copies, waits for them, and re-layouts: 26.3 us -> 12.3 us
  other arithmetic: 10.5 us -> 1.31 us
    pallas_call x0 -> x1, Pallas kernels: none -> 155 us  [on_device(): pl.pallas_call(kernel, out_shape=jax.ShapeDtypeStruct((patches, local, SD...]
    all_to_all x1 -> x0, blocking collectives: 67 us -> none  [on_device(): lax.all_to_all(analysis_own, 'mem', split_axis=0, concat_axis=1, tiled=True)]
    all_to_all x2 -> x0, waiting for transfers between devices: 59.8 us -> none  [the longest x1 37.3 us: on_device(): lax.all_to_all(flat_state, 'mem', split_axis=1, concat_axis=0, tiled=True)]
    dot_general x7 -> x0, matrix products: 22.7 us -> none  [the longest x1 7.36 us: inverse_root(): return jnp.dot(half_low, lower_iter, preferred_element_type=jnp.float32)]
    all_to_all x2 -> x0, starting transfers between devices: 16.9 us -> none  [the longest x1 10.9 us: on_device(): lax.all_to_all(ens_part, 'mem', split_axis=1, concat_axis=0, tiled=True)]
    unnamed x8 -> x2, local copies, waits for them, and re-layouts: 18.3 us -> 5.43 us
    convert_element_type x5 -> x1, other arithmetic: 7.46 us -> 1.31 us  [on_device(): side = jnp.concatenate([innovation.reshape(rows * cols, blk), obs_weight....]
    ppermute x2 -> x0, waiting for transfers between devices: 4.16 us -> none  [the longest x1 2.33 us: padded(): lax.ppermute(lax.slice_in_dim(block, 0, width, axis=dim), axis, backward)]
  transfers between devices with their start and end apart: 4 -> 0, of which waited for: 4 -> 0; matrix products, arithmetic and copies ran while one was open for 12% -> 0% of each run, Pallas kernels for 0% -> 0%
where the time goes in v1:
time: 171 us; the launch traced here: 170 us
  Pallas kernels  155 us (91%)
  local copies, waits for them, and re-layouts  12.3 us (7%)
    pallas_call x1, Pallas kernels, on_device(): pl.pallas_call(kernel, out_shape=jax.ShapeDtypeStruct((patches, local, SD...  155 us
    unnamed x2, local copies, waits for them, and re-layouts  5.43 us
    reshape x1, local copies, waits for them, and re-layouts, on_device(): return jnp.transpose(out, (1, 0, 2)).reshape(local, patches, 1, SDIM)  4.67 us

profile of v1, /device:TPU:8, one launch (start us, length us, event | category | flops | bytes accessed | tf_op | source)
XLA Modules:
  0.0 169.7 jit_solution(13223671977759476028)
XLA Ops:
  0.7 1.3 maximum_convert_fusion.side_ref
  2.0 0.8 copy.13
  2.7 0.6 reshape.27.loc_ref
  3.3 1.6 copy.12
  4.9 4.7 %copy.17 = bf16[32,32,1,1280]{3,0,1,2:T(8,128)(2,1)} copy(bf16[32,32,1,1280]{3,1,2,0:T(8,128)(2,1)} %param.13) | data formatting | bytes 5242880 | tf_op args[6]
  9.6 155.4 %analysis.1 = bf16[32,32,1280]{2,1,0:T(8,128)(2,1)} custom-call(bf16[16,32,128]{2,1,0:T(8,128)(2,1)} %bitcast.19, f32[32,128]{1,0:T(8,128)} %maximum_convert_fusion.side_ref, s32[128]{0:T(128)} %reshape.27.loc_ref, s32[1]{0:T(128)} %bitcast.16.cnt_ref, f32[4]{0:T(128)} %bitcast.23, bf16[32,32,1280]{2,1,0:T(8,128)(2,1)} %bitcast.18), custom_call_target="tpu_custom_call" | custom-call | tf_op jit(solution)/shard_map/analysis/pallas_call | solution.py:274
  165.0 4.7 %copy.15 = bf16[32,32,1,1280]{3,1,2,0:T(8,128)(2,1)} copy(bf16[32,32,1,1280]{3,0,1,2:T(8,128)(2,1)} %bitcast.17) | data formatting | bytes 5242880 | tf_op jit(solution)/shard_map/reshape | solution.py:300

commit v2 on v1

--- a/solution.py
+++ b/solution.py
@@ -17,27 +17,41 @@
 SLOTS = 4
 SDIM = 1280
 TILE = 256
-SELF_STEP = 4
+STARTS = (3, 6, 9, 14)
 
 
 def kernel(
-    obs_ref, side_ref, loc_ref, cnt_ref, tap_ref, state_ref, out_ref,
-    win, wside, pick, xfull, wgt, sfull, yroot, zroot, ynext, wmat, omat,
-    halo_send, halo_recv, side_send, side_recv,
-    ens_send, ens_recv, st_send, st_recv, out_send, out_recv, loc_sem,
+    ens_ref, innov_ref, wt_ref, loc_ref, cnt_ref, tap_ref, state_ref, out_ref,
+    win0, win1, win2, win3, win4, win5, win6, win7, wside, pick, xfull, wgt, snat, spat, sfull, yroot, zroot, ynext, wmat, omat,
+    ring_send, ring_recv, y_send, y_recv, side_send, side_recv,
+    ens_send, ens_recv, st_send, st_recv, out_send, out_recv, nat_sem, loc_sem,
 ):
+    wins = (win0, win1, win2, win3, win4, win5, win6, win7)
     me = lax.axis_index("mem")
     zc, xc = me // XN, me % XN
     yc = lax.axis_index("lon")
+    sign = 1 - 2 * lax.axis_index("lat")
 
     def peer(dz, dx):
         return ((zc + dz) % ZN) * XN + (xc + dx) % XN
 
     def offset(k):
-        dz = (4 + 3 * (k % ZN)) % ZN
-        return dz, (k // ZN + dz) % XN
-
+        lane = k % (ZN - 1)
+        dz = (4 + 3 * (lane + lane // 4)) % ZN
+        return dz, (k // (ZN - 1) + dz) % XN
+
+    far = (ZN - 1) * XN
     y_up, y_down = (yc + 1) % YN, (yc + YN - 1) % YN
+
+    group = 8
+    natural = []
+    for q in range(PEERS // group):
+        copy = pltpu.make_async_copy(
+            state_ref.at[:, pl.ds(q * group, group), :],
+            snat.at[:, pl.ds(q * group, group), :], nat_sem.at[q],
+        )
+        copy.start()
+        natural.append(copy)
 
     barrier = pltpu.get_barrier_semaphore()
 
@@ -48,51 +62,65 @@
         )
         return carry
 
-    lax.fori_loop(0, SELF_STEP, greet, 0)
-    lax.fori_loop(SELF_STEP + 1, PEERS, greet, 0)
+    lax.fori_loop(0, far, greet, 0)
+    for dx in range(1, XN):
+        pl.semaphore_signal(
+            barrier, inc=1, device_id={"mem": peer(0, dx)}, device_id_type=MESH
+        )
     for other in (y_up, y_down):
         pl.semaphore_signal(barrier, inc=1, device_id={"lon": other}, device_id_type=MESH)
+
+    wins[4][1] = jnp.swapaxes(ens_ref[...], 0, 1)
+    wside[1, 0:16] = innov_ref[...].astype(jnp.float32)
+    wside[1, 16:32] = wt_ref[...].astype(jnp.float32)
     pl.semaphore_wait(barrier, PEERS - 1 + 2)
 
-    halo = []
-    for slot, other in ((0, y_up), (2, y_down)):
-        i = slot // 2
-        halo.append(
+    def unit(r):
+        return (zc + sign * r + ZN) % ZN
+
+    def ring_copy(arm, s):
+        r = -s if arm == 0 else s
+        r_there = r - 1 if arm == 0 else r + 1
+        to = ((zc + sign * (1 - 2 * arm) + ZN) % ZN) * XN + xc
+        i = arm * 4 + s
+        return pltpu.make_async_remote_copy(
+            src_ref=wins[r + 4].at[1], dst_ref=wins[r_there + 4].at[1],
+            send_sem=ring_send.at[i], recv_sem=ring_recv.at[i],
+            device_id={"mem": to}, device_id_type=MESH,
+        )
+
+    def y_copies(r):
+        i = r + 4
+        return [
             pltpu.make_async_remote_copy(
-                src_ref=obs_ref, dst_ref=win.at[slot],
-                send_sem=halo_send.at[i], recv_sem=halo_recv.at[i],
+                src_ref=wins[i].at[1], dst_ref=wins[i].at[slot],
+                send_sem=y_send.at[slot // 2, i], recv_sem=y_recv.at[slot // 2, i],
                 device_id={"lon": other}, device_id_type=MESH,
             )
-        )
-        halo.append(
-            pltpu.make_async_remote_copy(
-                src_ref=side_ref, dst_ref=wside.at[slot],
-                send_sem=side_send.at[i], recv_sem=side_recv.at[i],
-                device_id={"lon": other}, device_id_type=MESH,
-            )
-        )
-    for copy in halo:
-        copy.start()
+            for slot, other in ((0, y_up), (2, y_down))
+        ]
+
+    sides = [
+        pltpu.make_async_remote_copy(
+            src_ref=wside.at[1], dst_ref=wside.at[slot],
+            send_sem=side_send.at[slot // 2], recv_sem=side_recv.at[slot // 2],
+            device_id={"lon": other}, device_id_type=MESH,
+        )
+        for slot, other in ((0, y_up), (2, y_down))
+    ]
 
     my_rows = pl.ds(pl.multiple_of(me * ROWS, ROWS), ROWS)
 
-    def state_copy(k):
-        dz, dx = offset(k)
+    def state_send(sem, dz, dx):
         to = peer(dz, dx)
         return pltpu.make_async_remote_copy(
-            src_ref=state_ref.at[to], dst_ref=sfull.at[my_rows],
-            send_sem=st_send.at[k], recv_sem=st_recv.at[k],
+            src_ref=spat.at[to], dst_ref=sfull.at[my_rows],
+            send_sem=st_send.at[sem], recv_sem=st_recv.at[sem],
             device_id={"mem": to}, device_id_type=MESH,
         )
 
-    def ens_copy(k):
-        dz, dx = offset(k)
-        to = peer(dz, dx)
-        return pltpu.make_async_remote_copy(
-            src_ref=pick.at[to], dst_ref=xfull.at[my_rows],
-            send_sem=ens_send.at[k], recv_sem=ens_recv.at[k],
-            device_id={"mem": to}, device_id_type=MESH,
-        )
+    def state_copy(k):
+        return state_send(k, *offset(k))
 
     def start(make):
         def body(k, carry):
@@ -112,47 +140,101 @@
             return carry
         return body
 
-    def others(body):
-        lax.fori_loop(0, SELF_STEP, body, 0)
-        lax.fori_loop(SELF_STEP + 1, PEERS, body, 0)
-
-    own_state = pltpu.make_async_copy(state_ref.at[me], sfull.at[my_rows], loc_sem.at[0])
+    ring = {(0, 0): ring_copy(0, 0), (1, 0): ring_copy(1, 0)}
+    rows_out = {0: y_copies(0)}
+    for copy in list(ring.values()) + rows_out[0] + sides:
+        copy.start()
+
+    lanes = 128
+    for q in range(PEERS // group):
+        natural[q].wait()
+
+        def relayout(t, carry):
+            cols = pl.ds(pl.multiple_of(t * lanes, lanes), lanes)
+            own = snat[:, q * group : (q + 1) * group, cols]
+            spat[q * group : (q + 1) * group, :, cols] = jnp.swapaxes(own, 0, 1)
+            return carry
+
+        lax.fori_loop(0, SDIM // lanes, relayout, 0)
+
+    own_state = pltpu.make_async_copy(spat.at[me], sfull.at[my_rows], loc_sem.at[0])
     own_state.start()
-    lax.fori_loop(0, SELF_STEP, start(state_copy), 0)
-
-    win[1] = obs_ref[...]
-    wside[1] = side_ref[...]
-    for copy in halo:
-        copy.wait()
+    near = [state_send(far + dx - 1, 0, dx) for dx in range(1, XN)]
+    for copy in near:
+        copy.start()
+
+    done = 0
+    for s in range(1, 5):
+        for arm in (0, 1):
+            if arm == 1 and s == 4:
+                continue
+            r = -s if arm == 0 else s
+            ring[arm, s - 1].wait_recv()
+            if s < 4 - arm:
+                ring[arm, s] = ring_copy(arm, s)
+                ring[arm, s].start()
+            rows_out[r] = y_copies(r)
+            for copy in rows_out[r]:
+                copy.start()
+        more = STARTS[s - 1]
+        lax.fori_loop(done, more, start(state_copy), 0)
+        done = more
 
     def block_index(number):
         row = (number * 43) >> 9
         col = number - row * 12
-        group = col >> 2
-        return group, row * 4 + (col - group * 4)
-
-    def pick_patch(p, carry):
-        for j in range(SLOTS):
-            group, block = block_index(loc_ref[p * SLOTS + j])
-            pick[p, :, j * BLK : (j + 1) * BLK] = win[group, block]
-        return carry
-
-    lax.fori_loop(0, PEERS, pick_patch, 0)
-    others(start(ens_copy))
-    xfull[my_rows, :] = pick[me]
-    lax.fori_loop(SELF_STEP + 1, PEERS, start(state_copy), 0)
+        third = col >> 2
+        return third, row * 4 + (col - third * 4)
+
+    listed = [
+        [block_index(loc_ref[j, zc * XN + (xc + dx) % XN]) for j in range(SLOTS)]
+        for dx in range(XN)
+    ]
+
+    def full_rows(r, x):
+        return pl.ds(pl.multiple_of((unit(r) * XN + x) * ROWS, ROWS), ROWS)
+
+    def ens_copy(dx, r):
+        i = r + 4
+        return pltpu.make_async_remote_copy(
+            src_ref=pick.at[dx - 1, i], dst_ref=xfull.at[full_rows(r, xc)],
+            send_sem=ens_send.at[dx - 1, i], recv_sem=ens_recv.at[dx - 1, i],
+            device_id={"mem": zc * XN + (xc + dx) % XN}, device_id_type=MESH,
+        )
+
+    picked = []
+    for r in (0, -1, 1, -2, 2, -3, 3, -4):
+        for copy in rows_out[r]:
+            copy.wait_recv()
+        for dx in (1, 2, 3, 0):
+            for j in range(SLOTS):
+                third, block = listed[dx][j]
+                tile = wins[r + 4][third, block]
+                cols = slice(j * BLK, (j + 1) * BLK)
+                if dx:
+                    pick[dx - 1, r + 4, :, cols] = tile
+                else:
+                    xfull[full_rows(r, xc), cols] = tile
+            if dx:
+                copy = ens_copy(dx, r)
+                copy.start()
+                picked.append(copy)
+    lax.fori_loop(done, far, start(state_copy), 0)
+    for copy in sides:
+        copy.wait_recv()
 
     count = cnt_ref[0]
     factors, innovs = [], []
     for j in range(SLOTS):
-        group, block = block_index(loc_ref[me * SLOTS + j])
+        third, block = listed[0][j]
         level = jnp.where(j < count, tap_ref[j], 0.0)
-        innovs.append(wside[group, pl.ds(block, 1), :])
-        factors.append(wside[group, pl.ds(block + 16, 1), :] * level)
+        innovs.append(wside[third, pl.ds(block, 1), :])
+        factors.append(wside[third, pl.ds(block + 16, 1), :] * level)
     factor = jnp.concatenate(factors, axis=1)
     innov = jnp.concatenate(innovs, axis=1)
 
-    others(wait_recv(ens_copy))
+    for copy in picked:
+        copy.wait_recv()
 
     drives = []
     total = jnp.zeros((1, 1), jnp.float32)
@@ -221,7 +303,9 @@
         full = yroot[rows, :].astype(jnp.float32) + mean[t * TILE : (t + 1) * TILE, 0:1]
         wmat[:, t * TILE : (t + 1) * TILE] = full.T.astype(jnp.bfloat16)
 
-    others(wait_recv(state_copy))
+    lax.fori_loop(0, far, wait_recv(state_copy), 0)
+    for copy in near:
+        copy.wait_recv()
     own_state.wait()
 
     def out_copy(k, dz, dx):
@@ -251,8 +335,12 @@
     own_out = pltpu.make_async_copy(omat.at[my_rows], out_ref.at[me], loc_sem.at[1])
     own_out.start()
 
-    others(wait_send(ens_copy))
-    others(wait_send(state_copy))
+    lax.fori_loop(0, far, wait_send(state_copy), 0)
+    early = list(ring.values()) + sides + near + picked
+    for copies in rows_out.values():
+        early += copies
+    for copy in early:
+        copy.wait_send()
     for copy in sends:
         copy.wait()
     own_out.wait()
@@ -260,12 +348,8 @@
 
 def on_device(ens_obs, innovation, obs_weight, loc_list, counts, taper, state):
     local, rows, cols, blk = ens_obs.shape
+    blocks = rows * cols
     patches = loc_list.shape[0]
-    obs = jnp.transpose(ens_obs, (1, 2, 0, 3)).reshape(rows * cols, local, blk)
-    side = jnp.concatenate(
-        [innovation.reshape(rows * cols, blk), obs_weight.reshape(rows * cols, blk)], axis=0
-    ).astype(jnp.float32)
-    by_patch = jnp.transpose(state.reshape(local, patches, SDIM), (1, 0, 2))
     vmem = pl.BlockSpec(memory_space=pltpu.VMEM)
     smem = pl.BlockSpec(memory_space=pltpu.SMEM)
     anywhere = pl.BlockSpec(memory_space=pl.ANY)
@@ -274,30 +358,57 @@
     out = pl.pallas_call(
         kernel,
         out_shape=jax.ShapeDtypeStruct((patches, local, SDIM), low),
-        in_specs=[vmem, vmem, smem, smem, smem, anywhere],
+        in_specs=[
+            vmem, vmem, vmem, smem, smem, smem,
+            pl.BlockSpec(memory_space=pltpu.MemorySpace.HBM),
+        ],
         out_specs=anywhere,
         scratch_shapes=[
-            pltpu.VMEM((3, rows * cols, local, blk), low),
-            pltpu.VMEM((3, 2 * rows * cols, blk), jnp.float32),
-            pltpu.VMEM((PEERS, local, OBS), low),
+            *[pltpu.VMEM((3, blocks, local, blk), low)] * ZN,
+            pltpu.VMEM((3, 2 * blocks, blk), jnp.float32),
+            pltpu.VMEM((XN - 1, ZN, local, OBS), low),
             pltpu.VMEM((MEMBERS, OBS), low),
             pltpu.VMEM((MEMBERS, OBS), low),
+            pltpu.VMEM((local, patches, SDIM), low),
+            pltpu.VMEM((patches, local, SDIM), low),
             pltpu.VMEM((MEMBERS, SDIM), low),
             pltpu.VMEM((MEMBERS, MEMBERS), low),
             pltpu.VMEM((MEMBERS, MEMBERS), low),
             pltpu.VMEM((MEMBERS, MEMBERS), low),
             pltpu.VMEM((MEMBERS, MEMBERS), low),
             pltpu.VMEM((MEMBERS, SDIM), low),
-            dma((2,)), dma((2,)), dma((2,)), dma((2,)),
-            dma((PEERS,)), dma((PEERS,)), dma((PEERS,)), dma((PEERS,)),
-            dma((PEERS,)), dma((PEERS,)), dma((2,)),
+            dma((7,)), dma((7,)), dma((2, ZN)), dma((2, ZN)), dma((2,)), dma((2,)),
+            dma((XN - 1, ZN)), dma((XN - 1, ZN)), dma((PEERS - 1,)), dma((PEERS - 1,)),
+            dma((PEERS,)), dma((PEERS,)), dma((4,)), dma((2,)),
         ],
         name="analysis",
         compiler_params=pltpu.CompilerParams(
-            collective_id=0, has_side_effects=True, vmem_limit_bytes=56 << 20
+            collective_id=0, has_side_effects=True, vmem_limit_bytes=36 << 20
         ),
-    )(obs, side, loc_list.reshape(-1), counts.reshape(-1), taper.reshape(-1), by_patch)
-    return jnp.transpose(out, (1, 0, 2)).reshape(local, patches, 1, SDIM)
+    )(
+        ens_obs.reshape(local, blocks, blk), innovation.reshape(blocks, blk),
+        obs_weight.reshape(blocks, blk), jnp.transpose(loc_list, (2, 1, 0)).reshape(SLOTS, patches),
+        counts.reshape(-1), taper.reshape(-1), state.reshape(local, patches, SDIM),
+    )
+    return by_member(out).reshape(local, patches, 1, SDIM)
+
+
+def by_member(patched):
+    patches, local, size = patched.shape
+    group = 8
+
+    def swap(x_ref, o_ref):
+        o_ref[...] = jnp.swapaxes(x_ref[...], 0, 1)
+
+    return pl.pallas_call(
+        swap,
+        grid=(patches // group,),
+        out_shape=jax.ShapeDtypeStruct((local, patches, size), patched.dtype),
+        in_specs=[pl.BlockSpec((group, local, size), lambda q: (q, 0, 0))],
+        out_specs=pl.BlockSpec((local, group, size), lambda q: (0, q, 0)),
+        name="by_member",
+        compiler_params=pltpu.CompilerParams(vmem_limit_bytes=12 << 20),
+    )(patched)
 
 
 def solution(mesh):

time: 171 us -> 153 us (0.89)
  Pallas kernels: 155 us -> 146 us
  local copies, waits for them, and re-layouts: 12.3 us -> 5.35 us
    pallas_call x1, Pallas kernels: 155 us -> 144 us  [on_device(): pl.pallas_call(kernel, out_shape=jax.ShapeDtypeStruct((patches, local, SD...]
    reshape x2 -> x0, local copies, waits for them, and re-layouts: 5.29 us -> none  [the longest x1 4.67 us: on_device(): return jnp.transpose(out, (1, 0, 2)).reshape(local, patches, 1, SDIM)]
    pallas_call x0 -> x1, Pallas kernels: none -> 2.23 us  [by_member(): pl.pallas_call(swap, grid=(patches // group,), out_shape=jax.ShapeDtypeSt...]
    unnamed x2 -> x12, local copies, waits for them, and re-layouts: 5.43 us -> 5.35 us
where the time goes in v2:
time: 153 us; the launch traced here: 152 us
  Pallas kernels  146 us (95%)
  local copies, waits for them, and re-layouts  5.35 us (3%)
    pallas_call x1, Pallas kernels, on_device(): pl.pallas_call(kernel, out_shape=jax.ShapeDtypeStruct((patches, local, SD...  144 us
    unnamed x12, local copies, waits for them, and re-layouts  5.35 us

profile of v2, /device:TPU:8, one launch (start us, length us, event | category | flops | bytes accessed | tf_op | source)
XLA Modules:
  0.0 152.2 jit_solution(15265559542499358596)
XLA Ops:
  0.7 0.0 copy-start
  0.7 1.7 %copy-done = bf16[32,32,1,1280]{3,1,2,0:T(8,128)(2,1)S(1)} copy-done((bf16[32,32,1,1280]{3,1,2,0:T(8,128)(2,1)S(1)}, bf16[32,32,1,1280]{3,1,2,0:T(8,128)(2,1)}, u32[]{:S(2)}) %copy-start) | copy-done | bytes 2621464
  2.4 0.0 copy-start.1
  2.4 0.9 copy-done.1
  3.3 0.0 copy-start.2
  3.3 0.7 copy-done.2
  4.0 0.0 copy-start.3
  4.0 0.7 copy-done.3
  4.7 0.0 copy-start.4
  4.7 0.7 copy-done.4
  5.4 0.0 copy-start.5
  5.4 0.7 copy-done.5
  6.0 143.9 %analysis.1.x_ref = bf16[32,32,1280]{2,1,0:T(8,128)(2,1)S(1)} custom-call(bf16[32,16,128]{2,1,0:T(8,128)(2,1)S(1)} %bitcast.14, bf16[16,128]{1,0:T(8,128)(2,1)S(1)} %bitcast.15, bf16[16,128]{1,0:T(8,128)(2,1)S(1)} %bitcast.16, s32[4,32]{1,0:T(4,128)S(1)} %bitcast.17, s32[1]{0:T(128)} %bitcast.12.cnt_ref, f32[4]{0:T(128)S(1)} %bitcast.18, ...), custom_call_target="tpu_custom_call" | custom-call | tf_op jit(solution)/shard_map/analysis/pallas_call | solution.py:358
  149.9 2.2 %by_member.1 = bf16[32,32,1280]{2,1,0:T(8,128)(2,1)} custom-call(bf16[32,32,1280]{2,1,0:T(8,128)(2,1)S(1)} %analysis.1.x_ref), custom_call_target="tpu_custom_call" | custom-call | tf_op jit(solution)/shard_map/by_member/pallas_call | solution.py:403
Async XLA Ops:
  0.7 1.7 %copy-start = (bf16[32,32,1,1280]{3,1,2,0:T(8,128)(2,1)S(1)}, bf16[32,32,1,1280]{3,1,2,0:T(8,128)(2,1)}, u32[]{:S(2)}) copy-start(bf16[32,32,1,1280]{3,1,2,0:T(8,128)(2,1)} %param.13) | copy-start | bytes 7864324
  2.4 0.9 copy-start.1
  3.3 0.7 copy-start.2
  4.0 0.7 copy-start.3
  4.7 0.7 copy-start.4
  5.4 0.7 copy-start.5

commit v3 on v2

--- a/solution.py
+++ b/solution.py
@@ -17,14 +17,15 @@
 SLOTS = 4
 SDIM = 1280
 TILE = 256
-STARTS = (3, 6, 9, 14)
+STARTS = (4, 8, 14, 24)
+PARTS = ((0, 768), (768, 512))
 
 
 def kernel(
     ens_ref, innov_ref, wt_ref, loc_ref, cnt_ref, tap_ref, state_ref, out_ref,
-    win0, win1, win2, win3, win4, win5, win6, win7, wside, pick, xfull, wgt, snat, spat, sfull, yroot, zroot, ynext, wmat, omat,
+    win0, win1, win2, win3, win4, win5, win6, win7, wside, pick, xfull, wgt, snat, spat, sfull, yroot, zroot, ynext, wmat, omat, obuf,
     ring_send, ring_recv, y_send, y_recv, side_send, side_recv,
-    ens_send, ens_recv, st_send, st_recv, out_send, out_recv, nat_sem, loc_sem,
+    ens_send, ens_recv, st_send, st_recv, out_send, out_recv, nat_sem, loc_sem, fin_sem,
 ):
     wins = (win0, win1, win2, win3, win4, win5, win6, win7)
     me = lax.axis_index("mem")
@@ -111,16 +112,17 @@
 
     my_rows = pl.ds(pl.multiple_of(me * ROWS, ROWS), ROWS)
 
-    def state_send(sem, dz, dx):
+    def state_send(part, sem, dz, dx):
         to = peer(dz, dx)
+        cols = pl.ds(*PARTS[part])
         return pltpu.make_async_remote_copy(
-            src_ref=spat.at[to], dst_ref=sfull.at[my_rows],
-            send_sem=st_send.at[sem], recv_sem=st_recv.at[sem],
+            src_ref=spat.at[to, :, cols], dst_ref=sfull.at[my_rows, cols],
+            send_sem=st_send.at[part, sem], recv_sem=st_recv.at[part, sem],
             device_id={"mem": to}, device_id_type=MESH,
         )
 
-    def state_copy(k):
-        return state_send(k, *offset(k))
+    def state_copy(part):
+        return lambda k: state_send(part, k, *offset(k))
 
     def start(make):
         def body(k, carry):
@@ -159,8 +161,8 @@
 
     own_state = pltpu.make_async_copy(spat.at[me], sfull.at[my_rows], loc_sem.at[0])
     own_state.start()
-    near = [state_send(far + dx - 1, 0, dx) for dx in range(1, XN)]
-    for copy in near:
+    near = [[state_send(h, far + dx - 1, 0, dx) for dx in range(1, XN)] for h in (0, 1)]
+    for copy in near[0]:
         copy.start()
 
     done = 0
@@ -177,7 +179,7 @@
             for copy in rows_out[r]:
                 copy.start()
         more = STARTS[s - 1]
-        lax.fori_loop(done, more, start(state_copy), 0)
+        lax.fori_loop(done, more, start(state_copy(0)), 0)
         done = more
 
     def block_index(number):
@@ -219,7 +221,10 @@
                 copy = ens_copy(dx, r)
                 copy.start()
                 picked.append(copy)
-    lax.fori_loop(done, far, start(state_copy), 0)
+    lax.fori_loop(done, far, start(state_copy(0)), 0)
+    for copy in near[1]:
+        copy.start()
+    lax.fori_loop(0, far, start(state_copy(1)), 0)
     for copy in sides:
         copy.wait_recv()
 
@@ -303,47 +308,70 @@
         full = yroot[rows, :].astype(jnp.float32) + mean[t * TILE : (t + 1) * TILE, 0:1]
         wmat[:, t * TILE : (t + 1) * TILE] = full.T.astype(jnp.bfloat16)
 
-    lax.fori_loop(0, far, wait_recv(state_copy), 0)
-    for copy in near:
-        copy.wait_recv()
+    def out_copy(part, k, dz, dx):
+        to = peer(dz, dx)
+        cols = pl.ds(*PARTS[part])
+        return pltpu.make_async_remote_copy(
+            src_ref=omat.at[pl.ds(pl.multiple_of(to * ROWS, ROWS), ROWS), cols],
+            dst_ref=obuf.at[me, :, cols],
+            send_sem=out_send.at[part, k], recv_sem=out_recv.at[part, k],
+            device_id={"mem": to}, device_id_type=MESH,
+        )
+
     own_state.wait()
-
-    def out_copy(k, dz, dx):
-        to = peer(dz, dx)
-        return pltpu.make_async_remote_copy(
-            src_ref=omat.at[pl.ds(pl.multiple_of(to * ROWS, ROWS), ROWS)],
-            dst_ref=out_ref.at[me],
-            send_sem=out_send.at[k], recv_sem=out_recv.at[k],
-            device_id={"mem": to}, device_id_type=MESH,
-        )
-
     plane = XN * ROWS
     sends = []
-    for pair in ((4, 3), (5, 2), (6, 1), (7, 0)):
-        starts = [pl.multiple_of(((zc + dz) % ZN) * plane, plane) for dz in pair]
-        left = jnp.concatenate([wmat[pl.ds(s, plane), :] for s in starts], axis=0)
-        block = jnp.dot(left, sfull[...], preferred_element_type=jnp.float32)
-        block = block.astype(jnp.bfloat16)
-        for i, s in enumerate(starts):
-            omat[pl.ds(s, plane), :] = block[i * plane : (i + 1) * plane, :]
-        for dx in range(XN):
-            for dz in pair:
-                if dz or dx:
-                    copy = out_copy(dz * XN + dx, dz, dx)
-                    copy.start()
-                    sends.append(copy)
-    own_out = pltpu.make_async_copy(omat.at[my_rows], out_ref.at[me], loc_sem.at[1])
-    own_out.start()
-
-    lax.fori_loop(0, far, wait_send(state_copy), 0)
-    early = list(ring.values()) + sides + near + picked
+    for part in (0, 1):
+        cols = pl.ds(*PARTS[part])
+        lax.fori_loop(0, far, wait_recv(state_copy(part)), 0)
+        for copy in near[part]:
+            copy.wait_recv()
+        for pair in ((4, 3), (5, 2), (6, 1), (7, 0)):
+            starts = [pl.multiple_of(((zc + dz) % ZN) * plane, plane) for dz in pair]
+            left = jnp.concatenate([wmat[pl.ds(s, plane), :] for s in starts], axis=0)
+            block = jnp.dot(left, sfull[:, cols], preferred_element_type=jnp.float32)
+            block = block.astype(jnp.bfloat16)
+            for i, s in enumerate(starts):
+                omat[pl.ds(s, plane), cols] = block[i * plane : (i + 1) * plane, :]
+            for dx in range(XN):
+                for dz in pair:
+                    if dz or dx:
+                        copy = out_copy(part, dz * XN + dx, dz, dx)
+                        copy.start()
+                        sends.append(copy)
+    obuf[me] = omat[my_rows, :]
+
+    stores = []
+    per_part = PEERS - 1
+    for part in (0, 1):
+        first, width = PARTS[part]
+        for copy in sends[part * per_part : (part + 1) * per_part]:
+            copy.wait_recv()
+        for q in range(PEERS // group):
+            pats = slice(q * group, (q + 1) * group)
+
+            def restore(t, carry):
+                cols = pl.ds(pl.multiple_of(first + t * lanes, lanes), lanes)
+                snat[:, pats, cols] = jnp.swapaxes(obuf[pats, :, cols], 0, 1)
+                return carry
+
+            lax.fori_loop(0, width // lanes, restore, 0)
+            copy = pltpu.make_async_copy(
+                snat.at[:, pats, pl.ds(first, width)], out_ref.at[:, pats, pl.ds(first, width)],
+                fin_sem.at[part, q],
+            )
+            copy.start()
+            stores.append(copy)
+
+    lax.fori_loop(0, far, wait_send(state_copy(0)), 0)
+    lax.fori_loop(0, far, wait_send(state_copy(1)), 0)
+    early = list(ring.values()) + sides + near[0] + near[1] + picked
     for copies in rows_out.values():
         early += copies
-    for copy in early:
+    for copy in early + sends:
         copy.wait_send()
-    for copy in sends:
+    for copy in stores:
         copy.wait()
-    own_out.wait()
 
 
 def on_device(ens_obs, innovation, obs_weight, loc_list, counts, taper, state):
@@ -357,7 +385,7 @@
     low = jnp.bfloat16
     out = pl.pallas_call(
         kernel,
-        out_shape=jax.ShapeDtypeStruct((patches, local, SDIM), low),
+        out_shape=jax.ShapeDtypeStruct((local, patches, SDIM), low),
         in_specs=[
             vmem, vmem, vmem, smem, smem, smem,
             pl.BlockSpec(memory_space=pltpu.MemorySpace.HBM),
@@ -377,38 +405,21 @@
             pltpu.VMEM((MEMBERS, MEMBERS), low),
             pltpu.VMEM((MEMBERS, MEMBERS), low),
             pltpu.VMEM((MEMBERS, SDIM), low),
+            pltpu.VMEM((patches, local, SDIM), low),
             dma((7,)), dma((7,)), dma((2, ZN)), dma((2, ZN)), dma((2,)), dma((2,)),
-            dma((XN - 1, ZN)), dma((XN - 1, ZN)), dma((PEERS - 1,)), dma((PEERS - 1,)),
-            dma((PEERS,)), dma((PEERS,)), dma((4,)), dma((2,)),
+            dma((XN - 1, ZN)), dma((XN - 1, ZN)), dma((2, PEERS - 1)), dma((2, PEERS - 1)),
+            dma((2, PEERS)), dma((2, PEERS)), dma((4,)), dma((2,)), dma((2, 4)),
         ],
         name="analysis",
         compiler_params=pltpu.CompilerParams(
-            collective_id=0, has_side_effects=True, vmem_limit_bytes=36 << 20
+            collective_id=0, has_side_effects=True, vmem_limit_bytes=60 << 20
         ),
     )(
         ens_obs.reshape(local, blocks, blk), innovation.reshape(blocks, blk),
         obs_weight.reshape(blocks, blk), jnp.transpose(loc_list, (2, 1, 0)).reshape(SLOTS, patches),
         counts.reshape(-1), taper.reshape(-1), state.reshape(local, patches, SDIM),
     )
-    return by_member(out).reshape(local, patches, 1, SDIM)
-
-
-def by_member(patched):
-    patches, local, size = patched.shape
-    group = 8
-
-    def swap(x_ref, o_ref):
-        o_ref[...] = jnp.swapaxes(x_ref[...], 0, 1)
-
-    return pl.pallas_call(
-        swap,
-        grid=(patches // group,),
-        out_shape=jax.ShapeDtypeStruct((local, patches, size), patched.dtype),
-        in_specs=[pl.BlockSpec((group, local, size), lambda q: (q, 0, 0))],
-        out_specs=pl.BlockSpec((local, group, size), lambda q: (0, q, 0)),
-        name="by_member",
-        compiler_params=pltpu.CompilerParams(vmem_limit_bytes=12 << 20),
-    )(patched)
+    return out.reshape(local, patches, 1, SDIM)
 
 
 def solution(mesh):

time: 153 us -> 146 us (0.954)
  Pallas kernels: 146 us -> 142 us
  local copies, waits for them, and re-layouts: 5.35 us -> 3.4 us
    pallas_call x2 -> x1, Pallas kernels: 146 us -> 142 us  [on_device(): pl.pallas_call(kernel, out_shape=jax.ShapeDtypeStruct((local, patches, SD...]
    unnamed x12 -> x1, local copies, waits for them, and re-layouts: 5.35 us -> 3.4 us
where the time goes in v3:
time: 146 us
  Pallas kernels  142 us (97%)
  local copies, waits for them, and re-layouts  3.4 us (2%)
    pallas_call x1, Pallas kernels, on_device(): pl.pallas_call(kernel, out_shape=jax.ShapeDtypeStruct((local, patches, SD...  142 us
    unnamed x1, local copies, waits for them, and re-layouts  3.4 us

profile of v3, /device:TPU:8, one launch (start us, length us, event | category | flops | bytes accessed | tf_op | source)
XLA Modules:
  0.0 145.7 jit_solution(2124146895437322875)
XLA Ops:
  0.7 141.6 %analysis.1 = bf16[32,32,1280]{2,1,0:T(8,128)(2,1)} custom-call(bf16[32,16,128]{2,1,0:T(8,128)(2,1)} %bitcast.15, bf16[16,128]{1,0:T(8,128)(2,1)} %bitcast.16, bf16[16,128]{1,0:T(8,128)(2,1)} %bitcast.17, s32[4,32]{1,0:T(4,128)} %bitcast.18, s32[1]{0:T(128)} %bitcast.12.cnt_ref, f32[4]{0:T(128)} %bitcast.19, bf16[32,32,1280]{2,1,0:T(8,128)(2,1)} %bitcast.14), custom_call_target="tpu_custom_call" | custom-call | tf_op jit(solution)/shard_map/analysis/pallas_call | solution.py:386
  142.3 3.4 %copy.11 = bf16[32,32,1,1280]{3,1,2,0:T(8,128)(2,1)} copy(bf16[32,32,1,1280]{3,1,2,0:T(8,128)(2,1)} %bitcast.13) | data formatting | bytes 5242880

commit v4 on v3

--- a/solution.py
+++ b/solution.py
@@ -18,14 +18,14 @@
 SDIM = 1280
 TILE = 256
 STARTS = (4, 8, 14, 24)
-PARTS = ((0, 768), (768, 512))
+PARTS = ((0, 896), (896, 384))
 
 
 def kernel(
     ens_ref, innov_ref, wt_ref, loc_ref, cnt_ref, tap_ref, state_ref, out_ref,
     win0, win1, win2, win3, win4, win5, win6, win7, wside, pick, xfull, wgt, snat, spat, sfull, yroot, zroot, ynext, wmat, omat, obuf,
     ring_send, ring_recv, y_send, y_recv, side_send, side_recv,
-    ens_send, ens_recv, st_send, st_recv, out_send, out_recv, nat_sem, loc_sem, fin_sem,
+    ens_send, ens_recv, st_send, st_recv, out_send, out_recv, nat_sem, loc_sem,
 ):
     wins = (win0, win1, win2, win3, win4, win5, win6, win7)
     me = lax.axis_index("mem")
@@ -341,7 +341,6 @@
                         sends.append(copy)
     obuf[me] = omat[my_rows, :]
 
-    stores = []
     per_part = PEERS - 1
     for part in (0, 1):
         first, width = PARTS[part]
@@ -352,16 +351,10 @@
 
             def restore(t, carry):
                 cols = pl.ds(pl.multiple_of(first + t * lanes, lanes), lanes)
-                snat[:, pats, cols] = jnp.swapaxes(obuf[pats, :, cols], 0, 1)
+                out_ref[:, pats, cols] = jnp.swapaxes(obuf[pats, :, cols], 0, 1)
                 return carry
 
             lax.fori_loop(0, width // lanes, restore, 0)
-            copy = pltpu.make_async_copy(
-                snat.at[:, pats, pl.ds(first, width)], out_ref.at[:, pats, pl.ds(first, width)],
-                fin_sem.at[part, q],
-            )
-            copy.start()
-            stores.append(copy)
 
     lax.fori_loop(0, far, wait_send(state_copy(0)), 0)
     lax.fori_loop(0, far, wait_send(state_copy(1)), 0)
@@ -370,8 +363,6 @@
         early += copies
     for copy in early + sends:
         copy.wait_send()
-    for copy in stores:
-        copy.wait()
 
 
 def on_device(ens_obs, innovation, obs_weight, loc_list, counts, taper, state):
@@ -385,12 +376,12 @@
     low = jnp.bfloat16
     out = pl.pallas_call(
         kernel,
-        out_shape=jax.ShapeDtypeStruct((local, patches, SDIM), low),
+        out_shape=pltpu.VMEM((local, patches, SDIM), low),
         in_specs=[
             vmem, vmem, vmem, smem, smem, smem,
             pl.BlockSpec(memory_space=pltpu.MemorySpace.HBM),
         ],
-        out_specs=anywhere,
+        out_specs=vmem,
         scratch_shapes=[
             *[pltpu.VMEM((3, blocks, local, blk), low)] * ZN,
             pltpu.VMEM((3, 2 * blocks, blk), jnp.float32),
@@ -408,11 +399,11 @@
             pltpu.VMEM((patches, local, SDIM), low),
             dma((7,)), dma((7,)), dma((2, ZN)), dma((2, ZN)), dma((2,)), dma((2,)),
             dma((XN - 1, ZN)), dma((XN - 1, ZN)), dma((2, PEERS - 1)), dma((2, PEERS - 1)),
-            dma((2, PEERS)), dma((2, PEERS)), dma((4,)), dma((2,)), dma((2, 4)),
+            dma((2, PEERS)), dma((2, PEERS)), dma((4,)), dma((2,)),
         ],
         name="analysis",
         compiler_params=pltpu.CompilerParams(
-            collective_id=0, has_side_effects=True, vmem_limit_bytes=60 << 20
+            collective_id=0, has_side_effects=True, vmem_limit_bytes=56 << 20
         ),
     )(
         ens_obs.reshape(local, blocks, blk), innovation.reshape(blocks, blk),

time: 146 us -> 144 us (0.986)
  local copies, waits for them, and re-layouts: 3.4 us -> 1.49 us
    unnamed x1, local copies, waits for them, and re-layouts: 3.4 us -> 1.49 us
where the time goes in v4:
time: 144 us
  Pallas kernels  141 us (98%)
  local copies, waits for them, and re-layouts  1.49 us (1%)
    pallas_call x1, Pallas kernels, on_device(): pl.pallas_call(kernel, out_shape=pltpu.VMEM((local, patches, SDIM), low),...  141 us

profile of v4, /device:TPU:8, one launch (start us, length us, event | category | flops | bytes accessed | tf_op | source)
XLA Modules:
  0.0 143.6 jit_solution(3364861384698020998)
XLA Ops:
  0.7 141.5 %analysis.1 = bf16[32,32,1280]{2,1,0:T(8,128)(2,1)S(1)} custom-call(bf16[32,16,128]{2,1,0:T(8,128)(2,1)} %bitcast.15, bf16[16,128]{1,0:T(8,128)(2,1)} %bitcast.16, bf16[16,128]{1,0:T(8,128)(2,1)} %bitcast.17, s32[4,32]{1,0:T(4,128)} %bitcast.18, s32[1]{0:T(128)} %bitcast.12.cnt_ref, f32[4]{0:T(128)} %bitcast.19, bf16[32,32,1280]{2,1,0:T(8,128)(2,1)} %bitcast.14), custom_call_target="tpu_custom_call" | custom-call | tf_op jit(solution)/shard_map/analysis/pallas_call | solution.py:377
  142.1 1.5 %copy.10 = bf16[32,32,1,1280]{3,1,2,0:T(8,128)(2,1)} copy(bf16[32,32,1,1280]{3,1,2,0:T(8,128)(2,1)S(1)} %bitcast.13) | data formatting | bytes 5242880

commit v5 on v4

--- a/solution.py
+++ b/solution.py
@@ -74,6 +74,18 @@
     wins[4][1] = jnp.swapaxes(ens_ref[...], 0, 1)
     wside[1, 0:16] = innov_ref[...].astype(jnp.float32)
     wside[1, 16:32] = wt_ref[...].astype(jnp.float32)
+    lanes = 128
+    for q in range(PEERS // group):
+        natural[q].wait()
+
+        def relayout(t, carry):
+            cols = pl.ds(pl.multiple_of(t * lanes, lanes), lanes)
+            own = snat[:, q * group : (q + 1) * group, cols]
+            spat[q * group : (q + 1) * group, :, cols] = jnp.swapaxes(own, 0, 1)
+            return carry
+
+        lax.fori_loop(0, SDIM // lanes, relayout, 0)
+
     pl.semaphore_wait(barrier, PEERS - 1 + 2)
 
     def unit(r):
@@ -146,18 +158,6 @@
     rows_out = {0: y_copies(0)}
     for copy in list(ring.values()) + rows_out[0] + sides:
         copy.start()
-
-    lanes = 128
-    for q in range(PEERS // group):
-        natural[q].wait()
-
-        def relayout(t, carry):
-            cols = pl.ds(pl.multiple_of(t * lanes, lanes), lanes)
-            own = snat[:, q * group : (q + 1) * group, cols]
-            spat[q * group : (q + 1) * group, :, cols] = jnp.swapaxes(own, 0, 1)
-            return carry
-
-        lax.fori_loop(0, SDIM // lanes, relayout, 0)
 
     own_state = pltpu.make_async_copy(spat.at[me], sfull.at[my_rows], loc_sem.at[0])
     own_state.start()

time: 144 us -> 144 us (level)
  no operation moved by 1% of the time
where the time goes in v5:
time: 144 us
  Pallas kernels  142 us (99%)
  local copies, waits for them, and re-layouts  1.49 us (1%)
    pallas_call x1, Pallas kernels, on_device(): pl.pallas_call(kernel, out_shape=pltpu.VMEM((local, patches, SDIM), low),...  142 us

profile of v5, /device:TPU:8, one launch (start us, length us, event | category | flops | bytes accessed | tf_op | source)
XLA Modules:
  0.0 143.7 jit_solution(339541087180112386)
XLA Ops:
  0.7 141.5 %analysis.1 = bf16[32,32,1280]{2,1,0:T(8,128)(2,1)S(1)} custom-call(bf16[32,16,128]{2,1,0:T(8,128)(2,1)} %bitcast.15, bf16[16,128]{1,0:T(8,128)(2,1)} %bitcast.16, bf16[16,128]{1,0:T(8,128)(2,1)} %bitcast.17, s32[4,32]{1,0:T(4,128)} %bitcast.18, s32[1]{0:T(128)} %bitcast.12.cnt_ref, f32[4]{0:T(128)} %bitcast.19, bf16[32,32,1280]{2,1,0:T(8,128)(2,1)} %bitcast.14), custom_call_target="tpu_custom_call" | custom-call | tf_op jit(solution)/shard_map/analysis/pallas_call | solution.py:377
  142.2 1.5 %copy.10 = bf16[32,32,1,1280]{3,1,2,0:T(8,128)(2,1)} copy(bf16[32,32,1,1280]{3,1,2,0:T(8,128)(2,1)S(1)} %bitcast.13) | data formatting | bytes 5242880

commit v6 on v4

--- a/solution.py
+++ b/solution.py
@@ -326,15 +326,16 @@
         lax.fori_loop(0, far, wait_recv(state_copy(part)), 0)
         for copy in near[part]:
             copy.wait_recv()
-        for pair in ((4, 3), (5, 2), (6, 1), (7, 0)):
+        for pair in ((4, 7), (2, 5), (3, 6), (1, 0)):
             starts = [pl.multiple_of(((zc + dz) % ZN) * plane, plane) for dz in pair]
             left = jnp.concatenate([wmat[pl.ds(s, plane), :] for s in starts], axis=0)
             block = jnp.dot(left, sfull[:, cols], preferred_element_type=jnp.float32)
             block = block.astype(jnp.bfloat16)
             for i, s in enumerate(starts):
                 omat[pl.ds(s, plane), cols] = block[i * plane : (i + 1) * plane, :]
-            for dx in range(XN):
+            for turn in range(XN):
                 for dz in pair:
+                    dx = (turn + dz) % XN
                     if dz or dx:
                         copy = out_copy(part, dz * XN + dx, dz, dx)
                         copy.start()

time: 144 us -> 144 us (level)
  no operation moved by 1% of the time
where the time goes in v6:
time: 144 us
  Pallas kernels  141 us (98%)
  local copies, waits for them, and re-layouts  1.49 us (1%)
    pallas_call x1, Pallas kernels, on_device(): pl.pallas_call(kernel, out_shape=pltpu.VMEM((local, patches, SDIM), low),...  141 us

profile of v6, /device:TPU:8, one launch (start us, length us, event | category | flops | bytes accessed | tf_op | source)
XLA Modules:
  0.0 143.6 jit_solution(8070656159719202339)
XLA Ops:
  0.7 141.4 %analysis.1 = bf16[32,32,1280]{2,1,0:T(8,128)(2,1)S(1)} custom-call(bf16[32,16,128]{2,1,0:T(8,128)(2,1)} %bitcast.15, bf16[16,128]{1,0:T(8,128)(2,1)} %bitcast.16, bf16[16,128]{1,0:T(8,128)(2,1)} %bitcast.17, s32[4,32]{1,0:T(4,128)} %bitcast.18, s32[1]{0:T(128)} %bitcast.12.cnt_ref, f32[4]{0:T(128)} %bitcast.19, bf16[32,32,1280]{2,1,0:T(8,128)(2,1)} %bitcast.14), custom_call_target="tpu_custom_call" | custom-call | tf_op jit(solution)/shard_map/analysis/pallas_call | solution.py:378
  142.1 1.5 %copy.10 = bf16[32,32,1,1280]{3,1,2,0:T(8,128)(2,1)} copy(bf16[32,32,1,1280]{3,1,2,0:T(8,128)(2,1)S(1)} %bitcast.13) | data formatting | bytes 5242880
